TPU v7x, 32 devices: a whole 2x2x4 slice. The times are simulated.
32 devices in a mesh: prow: 4 (over y, x), pcol: 8 (over z, core).
Axes of the slice: x: 2, y: 2, z: 4, core: 2. Of those that a mesh axis runs over, the one named last changes fastest.
Arguments:
- diag_block: float32 [128, 128], replicated, may hold values from 0 to 1.03, as said below
- panel: float32 [8192, 128], P(('prow', 'pcol')), may hold values from -0.2 to 1.2
- slab: float32 [8192, 2048], P('prow', 'pcol'), may hold values from -6 to 6
Outputs:
- slab_next: float32 [8192, 2048], P('prow', 'pcol')
- panel_factor: float32 [8192, 128], P(('prow', 'pcol'))
Inputs may be any that keep to these rules, and one draw needn't show every extreme that they name: diag_block is symmetric positive definite.
All inputs are finite; a program needn't handle non-finite values.
Results may differ from a plain program's by a relative error of at most 0.00091.
Values may be sent and summed in bfloat16 or wider, within the bound.
No kernel may reach another device: no remote copies, remote signals or barrier semaphores. Data moves between devices by JAX's collectives and lax.ppermute only.
A program may use at most 64 MiB of HBM per device.

v0:
```python
import jax
import jax.numpy as jnp
from jax import lax
from jax.sharding import PartitionSpec as P


def spread_2(x, axis, root):
    mine = lax.axis_index(axis) == root
    return lax.psum(jnp.where(mine, x, jnp.zeros_like(x)), axis)


def solve_rows(factor_block, rows_given):
    return lax.linalg.triangular_solve(
        factor_block, rows_given, left_side=False, lower=True, transpose_a=True
    )


def pick_blocks(source, leading, spread, panel_width, blocks_here):
    pieces = [
        lax.dynamic_slice_in_dim(
            source, (leading + position * spread) * panel_width, panel_width, 0
        )
        for position in range(blocks_here)
    ]
    return jnp.concatenate(pieces, 0)


def per_device(diag_block, panel, slab):
    prows = lax.axis_size("prow")
    pcols = lax.axis_size("pcol")
    factor_block = jnp.linalg.cholesky(diag_block)
    panel_width = factor_block.shape[0]
    spread = pcols // prows
    column_index = lax.axis_index("pcol")
    leading = column_index // prows
    blocks_here = slab.shape[1] // panel_width
    solved_rows = solve_rows(factor_block, panel)
    row_factor = lax.all_gather(solved_rows.astype(jnp.bfloat16), "pcol", axis=0, tiled=True)
    candidate = pick_blocks(row_factor, leading, spread, panel_width, blocks_here)
    column_factor = spread_2(candidate, "prow", column_index % prows)
    product = lax.dot_general(
        row_factor, column_factor, (((1,), (1,)), ((), ())), preferred_element_type=jnp.float32
    )
    return (slab - product, solved_rows)


def solution(mesh):
    placed = (P(), P(("prow", "pcol"), None), P("prow", "pcol"))
    return jax.shard_map(
        per_device,
        mesh=mesh,
        in_specs=placed,
        out_specs=(P("prow", "pcol"), P(("prow", "pcol"), None)),
        check_vma=False,
    )
```

profile of v0, /device:TPU:0, one launch (start us, length us, event | category | flops | bytes accessed | tf_op | source)
XLA Modules:
  0.0 102.2 jit_solution(17557626038271125850)
XLA Ops:
  7.2 0.0 copy-start
  7.2 0.0 copy-start.1
  7.2 0.0 all-reduce.2.cloned.1.call-start
  7.3 1.1 %copy.5 = f32[128,128]{0,1:T(8,128)S(1)} copy(f32[128,128]{1,0:T(8,128)} %param.3) | data formatting | bytes 131072 | tf_op args[0]
  8.3 0.9 fusion.2
  9.2 11.7 %cholesky.16 = f32[128,128]{1,0:T(8,128)S(1)} custom-call(f32[128,128]{1,0:T(8,128)S(1)} %fusion.2), custom_call_target="Cholesky" | custom-call | tf_op jit(solution)/shard_map/jit(cholesky)/cholesky | solution.py:31
  20.9 0.6 compare_reduce_fusion
  21.6 0.7 fusion
  22.3 9.8 %custom-call.6 = f32[1,128,128]{1,2,0:T(8,128)S(1)} custom-call(f32[1,128,128]{2,1,0:T(8,128)S(1)} %fusion), custom_call_target="InvertDiagBlocksLowerTriangular" | custom-call | tf_op jit(solution)/shard_map/triangular_solve | solution.py:13
  32.1 0.0 copy-done
  32.1 0.3 fusion.3
  32.4 16.5 %all_gather.3 = bf16[2048,128]{0,1:T(8,128)(2,1)S(1)} all-gather(bf16[256,128]{0,1:T(8,128)(2,1)S(1)} %get-tuple-element.6), channel_id=1, replica_groups=mesh['prow'=4,'pcol'=8] {'pcol'}, dimensions={0}, use_global_device_ids=true | all-gather | bytes 589824 | tf_op jit(solution)/shard_map/all_gather | solution.py:38
  48.9 0.6 maximum_select_fusion
  49.6 0.0 all-reduce.2.cloned.1.call-update
  49.6 0.8 copy.6
  50.4 42.3 %all-reduce.2.cloned.1.call-done = bf16[256,128]{0,1:T(8,128)(2,1)} async-done(((bf16[256,128]{0,1:T(8,128)(2,1)}), bf16[256,128]{0,1:T(8,128)(2,1)}) %all-reduce.2.cloned.1.call-update) | async-done | bytes 65552 | tf_op jit(solution)/shard_map/psum | solution.py:9
  92.7 0.0 copy-done.1
  92.7 2.6 %convolution_subtract_fusion = f32[2048,256]{1,0:T(8,128)} fusion(f32[2048,256]{1,0:T(8,128)S(1)} %copy-done.1, bf16[2048,128]{0,1:T(8,128)(2,1)S(1)} %all_gather.3, bf16[256,128]{0,1:T(8,128)(2,1)} %all-reduce.2.cloned.1.call-done), kind=kOutput, calls=%fused_computation | convolution fusion | flops 134742016 | bytes 4784128 | tf_op jit(solution)/shard_map/dot_general | solution.py:41
  (2 shorter events, 0.1 us)
Async XLA Ops:
  7.2 24.9 %copy-start = (f32[256,128]{1,0:T(8,128)S(1)}, f32[256,128]{1,0:T(8,128)}, u32[]{:S(2)}) copy-start(f32[256,128]{1,0:T(8,128)} %param.4) | copy-start | bytes 393220
  7.2 85.5 %copy-start.1 = (f32[2048,256]{1,0:T(8,128)S(1)}, f32[2048,256]{1,0:T(8,128)}, u32[]{:S(2)}) copy-start(f32[2048,256]{1,0:T(8,128)} %param.5) | copy-start | bytes 6291460
  7.2 85.5 %all-reduce.2.cloned.1.call-start = ((), (), s32[]{:S(2)}) async-start(), calls=%async_computation | async-start | bytes 131072 | tf_op jit(solution)/shard_map/psum | solution.py:9
Sparse Core Ops, SparseCore 0:
  49.7 42.9 all-reduce.1
where the time goes:
time: 102 us
  waiting for transfers between devices  42.3 us (41%)
  other arithmetic  24.4 us (24%)
  blocking collectives  16.5 us (16%)
  between operations  14.1 us (14%)
  matrix products  2.93 us (3%)
  local copies, waits for them, and re-layouts  1.86 us (2%)
    psum x1, waiting for transfers between devices, spread_2(): return lax.psum(jnp.where(mine, x, jnp.zeros_like(x)), axis)  42.3 us
    all_gather x1, blocking collectives, per_device(): lax.all_gather(solved_rows.astype(jnp.bfloat16), 'pcol', axis=0, tiled=True)  16.5 us
    another operation x3, other arithmetic, per_device(): factor_block = jnp.linalg.cholesky(diag_block)  12.4 us
    another operation x2, other arithmetic, solve_rows(): lax.linalg.triangular_solve(factor_block, rows_given, left_side=False, lo...  10.5 us
    dot_general x1, matrix products, per_device(): lax.dot_general(row_factor, column_factor, (((1,), (1,)), ((), ())), pref...  2.62 us
  transfers between devices with their start and end apart: 1, of which 1 were waited for; matrix products, arithmetic and copies ran while one was open for 1% of the time, Pallas kernels for 0%

commit v1 on v0

--- a/solution.py
+++ b/solution.py
@@ -4,9 +4,15 @@
 from jax.sharding import PartitionSpec as P
 
 
+def gather_and_add(block, axis):
+    terms = lax.all_gather(block, axis, axis=0, tiled=False)
+    summed = terms.sum(axis=0)
+    return summed
+
+
 def spread_2(x, axis, root):
     mine = lax.axis_index(axis) == root
-    return lax.psum(jnp.where(mine, x, jnp.zeros_like(x)), axis)
+    return gather_and_add(jnp.where(mine, x, jnp.zeros_like(x)), axis)
 
 
 def solve_rows(factor_block, rows_given):

time: 102 us -> 54.4 us (0.53)
  waiting for transfers between devices: 42.3 us -> 0 us
  between operations: 14.1 us -> 0.76 us
  blocking collectives: 16.5 us -> 25.5 us
    psum x1 -> x0, waiting for transfers between devices: 42.3 us -> none  [spread_2(): return lax.psum(jnp.where(mine, x, jnp.zeros_like(x)), axis)]
    all_gather x0 -> x1, blocking collectives: none -> 9 us  [gather_and_add(): terms = lax.all_gather(block, axis, axis=0, tiled=False)]
  transfers between devices with their start and end apart: 1 -> 0, of which waited for: 1 -> 0; matrix products, arithmetic and copies ran while one was open for 1% -> 0% of each run, Pallas kernels for 0% -> 0%
where the time goes in v1:
time: 54.4 us; the launch traced here: 54.2 us
  blocking collectives  25.5 us (47%)
  other arithmetic  23.8 us (44%)
  local copies, waits for them, and re-layouts  2.1 us (4%)
  matrix products  2.1 us (4%)
  between operations  0.76 us (1%)
    all_gather x1, blocking collectives, per_device(): lax.all_gather(solved_rows.astype(jnp.bfloat16), 'pcol', axis=0, tiled=True)  16.5 us
    another operation x3, other arithmetic, per_device(): factor_block = jnp.linalg.cholesky(diag_block)  12.4 us
    another operation x2, other arithmetic, solve_rows(): lax.linalg.triangular_solve(factor_block, rows_given, left_side=False, lo...  10.5 us
    all_gather x1, blocking collectives, gather_and_add(): terms = lax.all_gather(block, axis, axis=0, tiled=False)  9 us
    unnamed x6, local copies, waits for them, and re-layouts  1.85 us
    dot_general x1, matrix products, per_device(): lax.dot_general(row_factor, column_factor, (((1,), (1,)), ((), ())), pref...  1.79 us

profile of v1, /device:TPU:0, one launch (start us, length us, event | category | flops | bytes accessed | tf_op | source)
XLA Modules:
  0.0 54.2 jit_solution(12004026883969294216)
XLA Ops:
  0.6 0.0 copy-start
  0.6 0.0 copy-start.1
  0.7 1.1 %copy.10 = f32[128,128]{0,1:T(8,128)S(1)} copy(f32[128,128]{1,0:T(8,128)} %param.3) | data formatting | bytes 131072 | tf_op args[0]
  1.8 0.9 %fusion.2 = f32[128,128]{1,0:T(8,128)S(1)} fusion(f32[128,128]{1,0:T(8,128)} %param.3, f32[128,128]{0,1:T(8,128)S(1)} %copy.10), kind=kLoop, calls=%fused_computation.7 | loop fusion | flops 32768 | bytes 196608 | tf_op jit(solution)/shard_map/jit(cholesky)/div | solution.py:37
  2.6 11.7 %cholesky.16 = f32[128,128]{1,0:T(8,128)S(1)} custom-call(f32[128,128]{1,0:T(8,128)S(1)} %fusion.2), custom_call_target="Cholesky" | custom-call | tf_op jit(solution)/shard_map/jit(cholesky)/cholesky | solution.py:37
  14.4 0.6 %compare_reduce_fusion = pred[]{:T(512)} fusion(f32[128]{0:T(128)S(1)} %select_reduce_fusion), kind=kLoop, calls=%fused_computation.11 | loop fusion | flops 255 | bytes 513 | tf_op jit(solution)/shard_map/jit(cholesky)/cholesky | solution.py:37
  15.0 0.7 %fusion = f32[1,128,128]{2,1,0:T(8,128)S(1)} fusion(f32[128,128]{1,0:T(8,128)S(1)} %cholesky.16, pred[]{:T(512)} %compare_reduce_fusion), kind=kLoop, calls=%fused_computation.3 | loop fusion | flops 65536 | bytes 131073 | tf_op jit(solution)/shard_map/triangular_solve | solution.py:19
  15.7 9.8 %custom-call.6 = f32[1,128,128]{1,2,0:T(8,128)S(1)} custom-call(f32[1,128,128]{2,1,0:T(8,128)S(1)} %fusion), custom_call_target="InvertDiagBlocksLowerTriangular" | custom-call | tf_op jit(solution)/shard_map/triangular_solve | solution.py:19
  25.5 0.0 copy-done
  25.5 0.3 fusion.3
  25.8 0.8 %copy.14 = f32[256,128]{1,0:T(8,128)} copy(f32[256,128]{0,1:T(8,128)S(1)} %get-tuple-element.11) | data formatting | bytes 262144
  26.6 16.5 %all_gather.7 = bf16[2048,128]{0,1:T(8,128)(2,1)S(1)} all-gather(bf16[256,128]{0,1:T(8,128)(2,1)S(1)} %get-tuple-element.10), channel_id=1, replica_groups=mesh['prow'=4,'pcol'=8] {'pcol'}, dimensions={0}, use_global_device_ids=true | all-gather | bytes 589824 | tf_op jit(solution)/shard_map/all_gather | solution.py:44
  43.1 0.1 copy.11
  43.2 0.1 copy.12
  43.4 9.0 %all_gather.8 = bf16[4,256,128]{2,1,0:T(8,128)(2,1)S(1)} all-gather(bf16[1,256,128]{2,1,0:T(8,128)(2,1)S(1)} %maximum_select_fusion), channel_id=1, replica_groups=mesh['prow'=4,'pcol'=8] {'prow'}, dimensions={0}, use_global_device_ids=true | all-gather | bytes 327680 | tf_op jit(solution)/shard_map/all_gather | solution.py:8
  52.4 0.0 copy-done.1
  52.4 1.8 %convolution_subtract_fusion = f32[2048,256]{1,0:T(8,128)} fusion(f32[2048,256]{1,0:T(8,128)S(1)} %copy-done.1, bf16[2048,128]{0,1:T(8,128)(2,1)S(1)} %all_gather.7, bf16[256,128]{1,0:T(8,128)(2,1)S(1)} %reduce_sum.12), kind=kOutput, calls=%fused_computation | convolution fusion | flops 134742016 | bytes 4784128 | tf_op jit(solution)/shard_map/dot_general | solution.py:47
  (4 shorter events, 0.1 us)
Async XLA Ops:
  0.6 24.9 %copy-start = (f32[256,128]{1,0:T(8,128)S(1)}, f32[256,128]{1,0:T(8,128)}, u32[]{:S(2)}) copy-start(f32[256,128]{1,0:T(8,128)} %param.4) | copy-start | bytes 393220
  0.6 51.8 %copy-start.1 = (f32[2048,256]{1,0:T(8,128)S(1)}, f32[2048,256]{1,0:T(8,128)}, u32[]{:S(2)}) copy-start(f32[2048,256]{1,0:T(8,128)} %param.5) | copy-start | bytes 6291460
